TPU v7x, 128 devices: a whole 4x4x4 slice. The times are simulated.
128 devices in a mesh: tm: 32 (over y, x, core), blk: 4 (over z).
Axes of the slice: x: 4, y: 4, z: 4, core: 2. Of those that a mesh axis runs over, the one named last changes fastest.
Arguments:
- dynamics: float32 [256, 256], replicated
- dynamics_mask: int32 [8, 8], replicated, may hold values from 0 to 1, as said below
- obs_op: float32 [256, 256], replicated, may hold values from -0.375 to 0.375
- obs_mask: int32 [8, 8], replicated, may hold values from 0 to 1, as said below
- process_noise: float32 [256], replicated, may hold values from 0.0005 to 0.005
- initial_expectation: float32 [256], replicated, may hold values from -6 to 6
- filter_gains: float32 [512, 256, 256], P('tm', 'blk'), may hold values from -0.009765625 to 0.009765625
- observations: float32 [512, 256], P('tm'), may hold values from -6 to 6
- smooth_gains: float32 [512, 256, 256], P('tm', 'blk')
- filt_cov: float32 [512, 256, 256], P('tm', 'blk')
Outputs:
- smoothed_means: float32 [512, 256], P('tm', 'blk')
- smoothed_cov: float32 [512, 256, 256], P('tm', 'blk')
Inputs may be any that keep to these rules, and one draw needn't show every extreme that they name: `dynamics_mask`: diagonal blocks are 1. `obs_mask`: blocks with equal row and column index are 1.
All inputs are finite; a program needn't handle non-finite values.
Results may differ from a plain program's by a relative error of at most 0.0003.
Values sent between devices are 32-bit elements; how exact they have to be, the bound alone decides.
A program may use at most 256 MiB of HBM per device.

v0:
```python
import jax
import jax.numpy as jnp
from jax import lax
from jax.sharding import PartitionSpec as P

highest = lax.Precision.HIGHEST


def from_behind(block, axis, distance):
    devices = range(lax.axis_size(axis))
    route = [(i - distance, i) for i in devices if i - distance in devices]
    return lax.ppermute(block, axis, route)


def expand_mask(mask, row_total, col_total):
    row_block = row_total // mask.shape[0]
    col_block = col_total // mask.shape[1]
    return jnp.repeat(jnp.repeat(mask.astype(jnp.float32), row_block, axis=0), col_block, axis=1)


def matmul(left, right):
    return jnp.matmul(left, right, precision=highest)


def filter_join(earlier, latter):
    return (matmul(latter[0], earlier[0]), matmul(latter[0], earlier[1]) + latter[1])


def smooth_join(earlier, latter):
    gain_late = latter[0]
    return (
        matmul(gain_late, earlier[0]),
        matmul(matmul(gain_late, earlier[1]), gain_late.T) + latter[1],
        matmul(gain_late, earlier[2]) + latter[2],
    )


def pack_filter(parts):
    return jnp.concatenate([parts[0], parts[1][None, :]], axis=0)


def unpack_filter(packed, width):
    return (packed[:width], packed[width])


def pack_smooth(parts):
    return jnp.concatenate([parts[0], parts[1], parts[2][None, :]], axis=0)


def unpack_smooth(packed, width):
    return (packed[:width], packed[width : 2 * width], packed[2 * width])


def window_work(
    trans_map,
    process_noise,
    initial_expectation,
    transition_operators,
    step_shifts,
    gain_full,
    cov_full,
    is_final,
    filter_prefix,
    smooth_prefix,
):
    width = trans_map.shape[0]
    step_count = transition_operators.shape[0]
    final_step = jnp.logical_and(is_final, jnp.arange(step_count) == step_count - 1)
    gain_full = jnp.where(final_step[:, None, None], jnp.float32(0.0), gain_full)
    ident_map = jnp.eye(width, dtype=jnp.float32)
    zero_mat = jnp.zeros((width, width), jnp.float32)
    zero_vec = jnp.zeros((width,), jnp.float32)

    def window_filter(running, step_parts):
        return (filter_join(running, step_parts), None)

    filt_window = lax.scan(
        window_filter, (ident_map, zero_vec), (transition_operators, step_shifts)
    )[0]
    filt_before = filter_prefix(filt_window)
    mean_in = matmul(filt_before[0], initial_expectation) + filt_before[1]

    def filter_walk(current, step_parts):
        current = matmul(step_parts[0], current) + step_parts[1]
        return (current, current)

    filt_means = lax.scan(filter_walk, mean_in, (transition_operators, step_shifts))[1]
    predicted = matmul(matmul(trans_map, cov_full), trans_map.T) + jnp.diag(process_noise)
    gain_trans = jnp.swapaxes(gain_full, 1, 2)
    residual_cov = cov_full - matmul(matmul(gain_full, predicted), gain_trans)
    moved_means = jnp.einsum("ij,tj->ti", trans_map, filt_means, precision=highest)
    offsets = filt_means - jnp.einsum("tij,tj->ti", gain_full, moved_means, precision=highest)

    def window_smooth(running, step_parts):
        return (smooth_join(running, step_parts), None)

    smooth_window = lax.scan(
        window_smooth,
        (ident_map, zero_mat, zero_vec),
        (gain_full, residual_cov, offsets),
        reverse=True,
    )[0]
    smooth_after = smooth_prefix(smooth_window)

    def smooth_walk(current, step_parts):
        cov_next, mean_next = current
        gain_now, resid_now, offset_now = step_parts
        cov_now = matmul(matmul(gain_now, cov_next), gain_now.T) + resid_now
        current_mean = matmul(gain_now, mean_next) + offset_now
        return ((cov_now, current_mean), (current_mean, cov_now))

    return lax.scan(
        smooth_walk,
        (smooth_after[1], smooth_after[2]),
        (gain_full, residual_cov, offsets),
        reverse=True,
    )[1]


def per_device(
    dynamics,
    dynamics_mask,
    obs_op,
    obs_mask,
    process_noise,
    initial_expectation,
    filter_gains,
    observations,
    smooth_gains,
    filt_cov,
):
    width = dynamics.shape[0]
    obs_width = obs_op.shape[0]
    row_count = filter_gains.shape[1]
    row_start = lax.axis_index("blk") * row_count
    trans_map = dynamics * expand_mask(dynamics_mask, width, width)
    obs_map = obs_op * expand_mask(obs_mask, obs_width, width)
    obs_dyn = matmul(obs_map, trans_map)
    own_rows = lax.dynamic_slice_in_dim(trans_map, row_start, row_count, 0)
    map_rows = own_rows[None] - matmul(filter_gains, obs_dyn)
    shift_rows = jnp.einsum("tro,to->tr", filter_gains, observations, precision=highest)
    ident_map = jnp.eye(width, dtype=jnp.float32)
    zero_mat = jnp.zeros((width, width), jnp.float32)
    zero_vec = jnp.zeros((width,), jnp.float32)
    transition_operators, step_shifts, gain_full, cov_full = (
        lax.all_gather(map_rows, "blk", axis=1, tiled=True),
        lax.all_gather(shift_rows, "blk", axis=1, tiled=True),
        lax.all_gather(smooth_gains, "blk", axis=1, tiled=True),
        lax.all_gather(filt_cov, "blk", axis=1, tiled=True),
    )
    tm_index = lax.axis_index("tm")
    tm_count = lax.axis_size("tm")

    def before_filter(filt_window):

        def chain_filter(turn_no, running):
            arrived = from_behind(pack_filter(filter_join(running, filt_window)), "tm", 1)
            parts = unpack_filter(arrived, width)
            first_window = tm_index == 0
            return (
                jnp.where(first_window, ident_map, parts[0]),
                jnp.where(first_window, zero_vec, parts[1]),
            )

        return lax.fori_loop(0, tm_count - 1, chain_filter, (ident_map, zero_vec))

    def after_smooth(smooth_window):

        def chain_smooth(turn_no, running):
            arrived = from_behind(pack_smooth(smooth_join(running, smooth_window)), "tm", -1)
            parts = unpack_smooth(arrived, width)
            last_window = tm_index == tm_count - 1
            return (
                jnp.where(last_window, ident_map, parts[0]),
                jnp.where(last_window, zero_mat, parts[1]),
                jnp.where(last_window, zero_vec, parts[2]),
            )

        return lax.fori_loop(0, tm_count - 1, chain_smooth, (ident_map, zero_mat, zero_vec))

    means_out, cov_out = window_work(
        trans_map,
        process_noise,
        initial_expectation,
        transition_operators,
        step_shifts,
        gain_full,
        cov_full,
        tm_index == tm_count - 1,
        before_filter,
        after_smooth,
    )
    means_rows = lax.dynamic_slice_in_dim(means_out, row_start, row_count, 1)
    cov_rows = lax.dynamic_slice_in_dim(cov_out, row_start, row_count, 1)
    return (means_rows, cov_rows)


def solution(mesh):
    return jax.shard_map(
        per_device,
        mesh=mesh,
        in_specs=(
            P(),
            P(),
            P(),
            P(),
            P(),
            P(),
            P("tm", "blk", None),
            P("tm", None),
            P("tm", "blk", None),
            P("tm", "blk", None),
        ),
        out_specs=(P("tm", "blk"), P("tm", "blk", None)),
        check_vma=False,
    )
```

profile of v0, /device:TPU:7, one launch (start us, length us, event | category | flops | bytes accessed | tf_op | source)
XLA Modules:
  0.0 1111.3 jit_solution(17786515966806534478)
XLA Ops:
  28.2 36.9 %all-gather.9.cloned.1.call-done = f32[16,256,256]{2,1,0:T(8,128)} async-done(((f32[16,64,256]{2,1,0:T(8,128)}), f32[16,256,256]{2,1,0:T(8,128)}) %all-gather.9.cloned.1.call-update) | async-done | bytes 4194320 | tf_op jit(solution)/shard_map/all_gather | solution.py:146
  65.1 43.3 %while.99 = (s32[]{:T(128)}, f32[256,256]{1,0:T(8,128)S(1)}, f32[256]{0:T(256)S(1)}, f32[16,256,256]{2,1,0:T(8,128)}, f32[16,256]{1,0:T(8,128)S(1)}, /*index=5*/s32[]{:T(128)}, s32[]{:T(128)}) while((s32[]{:T(128)}, f32[256,256]{1,0:T(8,128)S(1)}, f32[256]{0:T(256)S(1)}, f32[16,256,256]{2,1,0:T(8,128)}, f32[16,256]{1,0:T(8,128)S(1)}, ...), condition=%wide.region_1.2_spmd.clone, body=%wide.region_0.1_spmd.clone.sunk | while | flops 202113536 | bytes 1583195 | solution.py:77
  108.5 329.0 %while.98 = (s32[]{:T(128)}, f32[256,256]{1,0:T(8,128)S(1)}, f32[256]{0:T(256)S(1)}, pred[]{:T(512)}, f32[256,256]{1,0:T(8,128)S(1)}, /*index=5*/f32[256]{0:T(256)S(1)}, s32[]{:T(128)}) while((s32[]{:T(128)}, f32[256,256]{1,0:T(8,128)S(1)}, f32[256]{0:T(256)S(1)}, pred[]{:T(512)}, f32[256,256]{1,0:T(8,128)S(1)}, ...), condition=%wide.region_3.4_spmd.clone, body=%wide.region_2.3_spmd.clone.sunk | while | flops 202375936 | bytes 3159159 | solution.py:165
  437.8 21.9 %while.96 = (s32[]{:T(128)}, f32[256]{0:T(256)S(1)}, f32[16,256]{1,0:T(8,128)S(1)}, f32[16,256,256]{2,1,0:T(8,128)}, f32[16,256]{1,0:T(8,128)S(1)}, /*index=5*/s32[]{:T(128)}, s32[]{:T(128)}) while((s32[]{:T(128)}, f32[256]{0:T(256)S(1)}, f32[16,256]{1,0:T(8,128)S(1)}, f32[16,256,256]{2,1,0:T(8,128)}, f32[16,256]{1,0:T(8,128)S(1)}, ...), condition=%wide.region_5.6_spmd, body=%wide.region_4.5_spmd.sunk | while | flops 786690 | bytes 271957 | solution.py:87
  487.6 88.0 %while.100 = (s32[]{:T(128)}, f32[256,256]{1,0:T(8,128)S(1)}, f32[256,256]{1,0:T(8,128)S(1)}, f32[256]{0:T(256)S(1)}, f32[16,256,256]{2,1,0:T(8,128)}, /*index=5...) while((s32[]{:T(128)}, f32[256,256]{1,0:T(8,128)S(1)}, ...), condition=%wide.region_7.8_spmd.clone, body=%wide.region_6.7_spmd.clone.sunk | while | flops 604897792 | bytes 3418252 | solution.py:97
  575.7 446.2 %while.101 = (s32[]{:T(128)}, f32[256,256]{1,0:T(8,128)S(1)}, f32[256,256]{1,0:T(8,128)S(1)}, f32[256]{0:T(256)S(1)}, pred[]{:T(512)}, /*index=5*/f32[256,256]{1...) while((s32[]{:T(128)}, f32[256,256]{1,0:T(8,128)S(1)}, ...), condition=%wide.region_9.10_spmd.clone, body=%wide.region_8.9_spmd.clone.sunk | while | flops 605422592 | bytes 7091353 | solution.py:179
  579.4 11.5 %collective-permute-done.1 = f32[513,256]{1,0:T(8,128)S(1)} collective-permute-done((f32[513,256]{1,0:T(8,128)S(1)}, f32[513,256]{1,0:T(8,128)S(1)}, u32[]{:S(2)}, u32[]{:S(2)}) %collective-permute-start.1) | collective-permute-done | bytes 525344 | tf_op jit(solution)/shard_map/while/body/eval_jaxpr/ppermute | solution.py:12
  594.5 10.8 collective-permute-done.1
  608.9 10.8 collective-permute-done.1
  623.2 10.8 collective-permute-done.1
  637.6 10.8 collective-permute-done.1
  652.0 10.8 collective-permute-done.1
  666.3 10.8 collective-permute-done.1
  680.7 10.8 collective-permute-done.1
  695.0 10.8 collective-permute-done.1
  738.1 10.8 collective-permute-done.1
  752.5 10.8 collective-permute-done.1
  781.2 10.8 collective-permute-done.1
  795.6 10.8 collective-permute-done.1
  809.9 10.8 collective-permute-done.1
  824.3 10.8 collective-permute-done.1
  853.0 10.8 collective-permute-done.1
  982.3 10.8 collective-permute-done.1
  1024.3 77.5 %while.97 = (s32[]{:T(128)}, f32[256,256]{1,0:T(8,128)S(1)}, f32[256]{0:T(256)S(1)}, f32[16,256]{1,0:T(8,128)S(1)}, f32[16,256,256]{2,1,0:T(8,128)}, /*index=5*/...) while((s32[]{:T(128)}, f32[256,256]{1,0:T(8,128)S(1)}, ...), condition=%wide.region_11.12_spmd, body=%wide.region_10.11_spmd.sunk | while | flops 403505408 | bytes 2369673 | solution.py:112
  (1001 shorter events, 868.9 us)
Async XLA Ops:
  7.2 58.0 %all-gather.9.cloned.1.call-start = ((), (), s32[]{:S(2)}) async-start(), calls=%async_computation.2 | async-start | bytes 5242880 | tf_op jit(solution)/shard_map/all_gather | solution.py:146
  14.2 445.7 %all-gather.5.cloned.1.call-start = ((), (), s32[]{:S(2)}) async-start(), calls=%async_computation | async-start | bytes 5242880 | tf_op jit(solution)/shard_map/all_gather | solution.py:148
  15.0 453.4 %all-gather.7.cloned.1.call-start = ((), (), s32[]{:S(2)}) async-start(), calls=%async_computation.1 | async-start | bytes 5242880 | tf_op jit(solution)/shard_map/all_gather | solution.py:149
  577.5 13.4 %collective-permute-start.1 = (f32[513,256]{1,0:T(8,128)S(1)}, f32[513,256]{1,0:T(8,128)S(1)}, u32[]{:S(2)}, u32[]{:S(2)}) collective-permute-start(f32[513,256]{1,0:T(8,128)S(1)} %pad_maximum_fusion.5), channel_id=1, source_target_pairs={{4,0},{8,4},{12,8},{16,12},{20,16},{24,20},{28,24},{32,28},{36,32}... | collective-permute-start | bytes 1575944 | tf_op jit(solution)/shard_map/while/body/eval_jaxpr/ppermute | solution.py:12
  592.6 12.7 %collective-permute-start.1 = (f32[513,256]{1,0:T(8,128)S(1)}, f32[513,256]{1,0:T(8,128)S(1)}, u32[]{:S(2)}, u32[]{:S(2)}) collective-permute-start(f32[513,256]{1,0:T(8,128)S(1)} %pad_maximum_fusion.5), channel_id=1, source_target_pairs={{4,0},{8,4},{12,8},{16,12},{20,16},{24,20},{28,24},{32,28},{36,32}... | collective-permute-start | bytes 1575944 | tf_op jit(solution)/shard_map/while/body/eval_jaxpr/ppermute | solution.py:12
  606.9 12.7 %collective-permute-start.1 = (f32[513,256]{1,0:T(8,128)S(1)}, f32[513,256]{1,0:T(8,128)S(1)}, u32[]{:S(2)}, u32[]{:S(2)}) collective-permute-start(f32[513,256]{1,0:T(8,128)S(1)} %pad_maximum_fusion.5), channel_id=1, source_target_pairs={{4,0},{8,4},{12,8},{16,12},{20,16},{24,20},{28,24},{32,28},{36,32}... | collective-permute-start | bytes 1575944 | tf_op jit(solution)/shard_map/while/body/eval_jaxpr/ppermute | solution.py:12
  621.3 12.7 %collective-permute-start.1 = (f32[513,256]{1,0:T(8,128)S(1)}, f32[513,256]{1,0:T(8,128)S(1)}, u32[]{:S(2)}, u32[]{:S(2)}) collective-permute-start(f32[513,256]{1,0:T(8,128)S(1)} %pad_maximum_fusion.5), channel_id=1, source_target_pairs={{4,0},{8,4},{12,8},{16,12},{20,16},{24,20},{28,24},{32,28},{36,32}... | collective-permute-start | bytes 1575944 | tf_op jit(solution)/shard_map/while/body/eval_jaxpr/ppermute | solution.py:12
  635.7 12.7 %collective-permute-start.1 = (f32[513,256]{1,0:T(8,128)S(1)}, f32[513,256]{1,0:T(8,128)S(1)}, u32[]{:S(2)}, u32[]{:S(2)}) collective-permute-start(f32[513,256]{1,0:T(8,128)S(1)} %pad_maximum_fusion.5), channel_id=1, source_target_pairs={{4,0},{8,4},{12,8},{16,12},{20,16},{24,20},{28,24},{32,28},{36,32}... | collective-permute-start | bytes 1575944 | tf_op jit(solution)/shard_map/while/body/eval_jaxpr/ppermute | solution.py:12
  650.0 12.7 %collective-permute-start.1 = (f32[513,256]{1,0:T(8,128)S(1)}, f32[513,256]{1,0:T(8,128)S(1)}, u32[]{:S(2)}, u32[]{:S(2)}) collective-permute-start(f32[513,256]{1,0:T(8,128)S(1)} %pad_maximum_fusion.5), channel_id=1, source_target_pairs={{4,0},{8,4},{12,8},{16,12},{20,16},{24,20},{28,24},{32,28},{36,32}... | collective-permute-start | bytes 1575944 | tf_op jit(solution)/shard_map/while/body/eval_jaxpr/ppermute | solution.py:12
  664.4 12.7 %collective-permute-start.1 = (f32[513,256]{1,0:T(8,128)S(1)}, f32[513,256]{1,0:T(8,128)S(1)}, u32[]{:S(2)}, u32[]{:S(2)}) collective-permute-start(f32[513,256]{1,0:T(8,128)S(1)} %pad_maximum_fusion.5), channel_id=1, source_target_pairs={{4,0},{8,4},{12,8},{16,12},{20,16},{24,20},{28,24},{32,28},{36,32}... | collective-permute-start | bytes 1575944 | tf_op jit(solution)/shard_map/while/body/eval_jaxpr/ppermute | solution.py:12
  678.7 12.7 %collective-permute-start.1 = (f32[513,256]{1,0:T(8,128)S(1)}, f32[513,256]{1,0:T(8,128)S(1)}, u32[]{:S(2)}, u32[]{:S(2)}) collective-permute-start(f32[513,256]{1,0:T(8,128)S(1)} %pad_maximum_fusion.5), channel_id=1, source_target_pairs={{4,0},{8,4},{12,8},{16,12},{20,16},{24,20},{28,24},{32,28},{36,32}... | collective-permute-start | bytes 1575944 | tf_op jit(solution)/shard_map/while/body/eval_jaxpr/ppermute | solution.py:12
  693.1 12.7 %collective-permute-start.1 = (f32[513,256]{1,0:T(8,128)S(1)}, f32[513,256]{1,0:T(8,128)S(1)}, u32[]{:S(2)}, u32[]{:S(2)}) collective-permute-start(f32[513,256]{1,0:T(8,128)S(1)} %pad_maximum_fusion.5), channel_id=1, source_target_pairs={{4,0},{8,4},{12,8},{16,12},{20,16},{24,20},{28,24},{32,28},{36,32}... | collective-permute-start | bytes 1575944 | tf_op jit(solution)/shard_map/while/body/eval_jaxpr/ppermute | solution.py:12
  707.5 12.7 %collective-permute-start.1 = (f32[513,256]{1,0:T(8,128)S(1)}, f32[513,256]{1,0:T(8,128)S(1)}, u32[]{:S(2)}, u32[]{:S(2)}) collective-permute-start(f32[513,256]{1,0:T(8,128)S(1)} %pad_maximum_fusion.5), channel_id=1, source_target_pairs={{4,0},{8,4},{12,8},{16,12},{20,16},{24,20},{28,24},{32,28},{36,32}... | collective-permute-start | bytes 1575944 | tf_op jit(solution)/shard_map/while/body/eval_jaxpr/ppermute | solution.py:12
  721.8 12.7 %collective-permute-start.1 = (f32[513,256]{1,0:T(8,128)S(1)}, f32[513,256]{1,0:T(8,128)S(1)}, u32[]{:S(2)}, u32[]{:S(2)}) collective-permute-start(f32[513,256]{1,0:T(8,128)S(1)} %pad_maximum_fusion.5), channel_id=1, source_target_pairs={{4,0},{8,4},{12,8},{16,12},{20,16},{24,20},{28,24},{32,28},{36,32}... | collective-permute-start | bytes 1575944 | tf_op jit(solution)/shard_map/while/body/eval_jaxpr/ppermute | solution.py:12
  736.2 12.7 %collective-permute-start.1 = (f32[513,256]{1,0:T(8,128)S(1)}, f32[513,256]{1,0:T(8,128)S(1)}, u32[]{:S(2)}, u32[]{:S(2)}) collective-permute-start(f32[513,256]{1,0:T(8,128)S(1)} %pad_maximum_fusion.5), channel_id=1, source_target_pairs={{4,0},{8,4},{12,8},{16,12},{20,16},{24,20},{28,24},{32,28},{36,32}... | collective-permute-start | bytes 1575944 | tf_op jit(solution)/shard_map/while/body/eval_jaxpr/ppermute | solution.py:12
  750.6 12.7 %collective-permute-start.1 = (f32[513,256]{1,0:T(8,128)S(1)}, f32[513,256]{1,0:T(8,128)S(1)}, u32[]{:S(2)}, u32[]{:S(2)}) collective-permute-start(f32[513,256]{1,0:T(8,128)S(1)} %pad_maximum_fusion.5), channel_id=1, source_target_pairs={{4,0},{8,4},{12,8},{16,12},{20,16},{24,20},{28,24},{32,28},{36,32}... | collective-permute-start | bytes 1575944 | tf_op jit(solution)/shard_map/while/body/eval_jaxpr/ppermute | solution.py:12
  764.9 12.7 %collective-permute-start.1 = (f32[513,256]{1,0:T(8,128)S(1)}, f32[513,256]{1,0:T(8,128)S(1)}, u32[]{:S(2)}, u32[]{:S(2)}) collective-permute-start(f32[513,256]{1,0:T(8,128)S(1)} %pad_maximum_fusion.5), channel_id=1, source_target_pairs={{4,0},{8,4},{12,8},{16,12},{20,16},{24,20},{28,24},{32,28},{36,32}... | collective-permute-start | bytes 1575944 | tf_op jit(solution)/shard_map/while/body/eval_jaxpr/ppermute | solution.py:12
  779.3 12.7 %collective-permute-start.1 = (f32[513,256]{1,0:T(8,128)S(1)}, f32[513,256]{1,0:T(8,128)S(1)}, u32[]{:S(2)}, u32[]{:S(2)}) collective-permute-start(f32[513,256]{1,0:T(8,128)S(1)} %pad_maximum_fusion.5), channel_id=1, source_target_pairs={{4,0},{8,4},{12,8},{16,12},{20,16},{24,20},{28,24},{32,28},{36,32}... | collective-permute-start | bytes 1575944 | tf_op jit(solution)/shard_map/while/body/eval_jaxpr/ppermute | solution.py:12
  793.6 12.7 %collective-permute-start.1 = (f32[513,256]{1,0:T(8,128)S(1)}, f32[513,256]{1,0:T(8,128)S(1)}, u32[]{:S(2)}, u32[]{:S(2)}) collective-permute-start(f32[513,256]{1,0:T(8,128)S(1)} %pad_maximum_fusion.5), channel_id=1, source_target_pairs={{4,0},{8,4},{12,8},{16,12},{20,16},{24,20},{28,24},{32,28},{36,32}... | collective-permute-start | bytes 1575944 | tf_op jit(solution)/shard_map/while/body/eval_jaxpr/ppermute | solution.py:12
  808.0 12.7 %collective-permute-start.1 = (f32[513,256]{1,0:T(8,128)S(1)}, f32[513,256]{1,0:T(8,128)S(1)}, u32[]{:S(2)}, u32[]{:S(2)}) collective-permute-start(f32[513,256]{1,0:T(8,128)S(1)} %pad_maximum_fusion.5), channel_id=1, source_target_pairs={{4,0},{8,4},{12,8},{16,12},{20,16},{24,20},{28,24},{32,28},{36,32}... | collective-permute-start | bytes 1575944 | tf_op jit(solution)/shard_map/while/body/eval_jaxpr/ppermute | solution.py:12
  822.4 12.7 %collective-permute-start.1 = (f32[513,256]{1,0:T(8,128)S(1)}, f32[513,256]{1,0:T(8,128)S(1)}, u32[]{:S(2)}, u32[]{:S(2)}) collective-permute-start(f32[513,256]{1,0:T(8,128)S(1)} %pad_maximum_fusion.5), channel_id=1, source_target_pairs={{4,0},{8,4},{12,8},{16,12},{20,16},{24,20},{28,24},{32,28},{36,32}... | collective-permute-start | bytes 1575944 | tf_op jit(solution)/shard_map/while/body/eval_jaxpr/ppermute | solution.py:12
  836.7 12.7 %collective-permute-start.1 = (f32[513,256]{1,0:T(8,128)S(1)}, f32[513,256]{1,0:T(8,128)S(1)}, u32[]{:S(2)}, u32[]{:S(2)}) collective-permute-start(f32[513,256]{1,0:T(8,128)S(1)} %pad_maximum_fusion.5), channel_id=1, source_target_pairs={{4,0},{8,4},{12,8},{16,12},{20,16},{24,20},{28,24},{32,28},{36,32}... | collective-permute-start | bytes 1575944 | tf_op jit(solution)/shard_map/while/body/eval_jaxpr/ppermute | solution.py:12
  851.1 12.7 %collective-permute-start.1 = (f32[513,256]{1,0:T(8,128)S(1)}, f32[513,256]{1,0:T(8,128)S(1)}, u32[]{:S(2)}, u32[]{:S(2)}) collective-permute-start(f32[513,256]{1,0:T(8,128)S(1)} %pad_maximum_fusion.5), channel_id=1, source_target_pairs={{4,0},{8,4},{12,8},{16,12},{20,16},{24,20},{28,24},{32,28},{36,32}... | collective-permute-start | bytes 1575944 | tf_op jit(solution)/shard_map/while/body/eval_jaxpr/ppermute | solution.py:12
  980.3 12.7 %collective-permute-start.1 = (f32[513,256]{1,0:T(8,128)S(1)}, f32[513,256]{1,0:T(8,128)S(1)}, u32[]{:S(2)}, u32[]{:S(2)}) collective-permute-start(f32[513,256]{1,0:T(8,128)S(1)} %pad_maximum_fusion.5), channel_id=1, source_target_pairs={{4,0},{8,4},{12,8},{16,12},{20,16},{24,20},{28,24},{32,28},{36,32}... | collective-permute-start | bytes 1575944 | tf_op jit(solution)/shard_map/while/body/eval_jaxpr/ppermute | solution.py:12
  (52 other events, 940.8 us)
Sparse Core Ops, SparseCore 0:
  14.3 50.7 all-gather.8
  66.8 48.9 all-gather.4
  117.5 48.4 all-gather.6
where the time goes:
time: 1120 us; the launch traced here: 1110 us
  waiting for transfers between devices  478 us (43%)
  matrix products  317 us (28%)
  starting transfers between devices  258 us (23%)
  local copies, waits for them, and re-layouts  16.4 us (1%)
  between operations  14.1 us (1%)
    ppermute x62, waiting for transfers between devices, from_behind(): return lax.ppermute(block, axis, route)  439 us
    dot_general x353, matrix products, matmul(): return jnp.matmul(left, right, precision=highest)  312 us
    ppermute x62, starting transfers between devices, from_behind(): return lax.ppermute(block, axis, route)  258 us
    all_gather x1, waiting for transfers between devices, per_device(): lax.all_gather(map_rows, 'blk', axis=1, tiled=True)  36.9 us
  transfers between devices with their start and end apart: 65, of which 63 were waited for; matrix products, arithmetic and copies ran while one was open for 9% of the time, Pallas kernels for 0%

commit v1 on v0

--- a/solution.py
+++ b/solution.py
@@ -4,6 +4,13 @@
 from jax.sharding import PartitionSpec as P
 
 highest = lax.Precision.HIGHEST
+
+
+def all_by_exchange(array, mesh_axis, along):
+    size = lax.axis_size(mesh_axis)
+    shards = jnp.stack([array for _ in range(size)])
+    shards = lax.all_to_all(shards, mesh_axis, split_axis=0, concat_axis=0)
+    return jnp.concatenate(shards, axis=along)
 
 
 def from_behind(block, axis, distance):
@@ -143,7 +150,7 @@
     zero_mat = jnp.zeros((width, width), jnp.float32)
     zero_vec = jnp.zeros((width,), jnp.float32)
     transition_operators, step_shifts, gain_full, cov_full = (
-        lax.all_gather(map_rows, "blk", axis=1, tiled=True),
+        all_by_exchange(map_rows, "blk", 1),
         lax.all_gather(shift_rows, "blk", axis=1, tiled=True),
         lax.all_gather(smooth_gains, "blk", axis=1, tiled=True),
         lax.all_gather(filt_cov, "blk", axis=1, tiled=True),

time: 1120 us -> 1170 us (1.045)
  blocking collectives: 10.5 us -> 84.3 us
  waiting for transfers between devices: 478 us -> 441 us
    all_gather x1, blocking collectives: 10.5 us -> 84.3 us  [per_device(): lax.all_gather(shift_rows, 'blk', axis=1, tiled=True)]
    all_gather x1 -> x0, waiting for transfers between devices: 36.9 us -> none  [per_device(): lax.all_gather(map_rows, 'blk', axis=1, tiled=True)]
  transfers between devices with their start and end apart: 65 -> 65, of which waited for: 63 -> 62; matrix products, arithmetic and copies ran while one was open for 9% -> 9% of each run, Pallas kernels for 0% -> 0%
where the time goes in v1:
time: 1170 us; the launch traced here: 1160 us
  waiting for transfers between devices  441 us (38%)
  matrix products  316 us (27%)
  starting transfers between devices  266 us (23%)
  blocking collectives  84.3 us (7%)
  local copies, waits for them, and re-layouts  23.3 us (2%)
  between operations  14.4 us (1%)
    ppermute x62, waiting for transfers between devices, from_behind(): return lax.ppermute(block, axis, route)  439 us
    dot_general x353, matrix products, matmul(): return jnp.matmul(left, right, precision=highest)  311 us
    ppermute x62, starting transfers between devices, from_behind(): return lax.ppermute(block, axis, route)  261 us
    all_gather x1, blocking collectives, per_device(): lax.all_gather(shift_rows, 'blk', axis=1, tiled=True)  84.3 us
  transfers between devices with their start and end apart: 65, of which 62 were waited for; matrix products, arithmetic and copies ran while one was open for 9% of the time, Pallas kernels for 0%

profile of v1, /device:TPU:7, one launch (start us, length us, event | category | flops | bytes accessed | tf_op | source)
XLA Modules:
  0.0 1161.6 jit_solution(7024248650072272359)
XLA Ops:
  23.3 84.3 %all-gather = f32[4,64,16]{1,2,0:T(8,128)S(1)} all-gather(f32[1,64,16]{1,2,0:T(8,128)S(1)} %bitcast.262), channel_id=1, replica_groups=mesh['tm'=32,'blk'=4] {'blk'}, dimensions={0}, use_global_device_ids=true | all-gather | bytes 20480 | tf_op jit(solution)/shard_map/all_gather | solution.py:154
  112.5 43.4 %while.99 = (s32[]{:T(128)}, f32[256,256]{1,0:T(8,128)S(1)}, f32[256]{0:T(256)S(1)}, f32[16,256,256]{2,1,0:T(8,128)}, f32[16,256]{1,0:T(8,128)S(1)}, /*index=5*/s32[]{:T(128)}, s32[]{:T(128)}) while((s32[]{:T(128)}, f32[256,256]{1,0:T(8,128)S(1)}, f32[256]{0:T(256)S(1)}, f32[16,256,256]{2,1,0:T(8,128)}, f32[16,256]{1,0:T(8,128)S(1)}, ...), condition=%wide.region_1.2_spmd.clone, body=%wide.region_0.1_spmd.clone.sunk | while | flops 202113536 | bytes 1583195 | solution.py:84
  156.0 331.5 %while.98 = (s32[]{:T(128)}, f32[256,256]{1,0:T(8,128)S(1)}, f32[256]{0:T(256)S(1)}, pred[]{:T(512)}, f32[256,256]{1,0:T(8,128)S(1)}, /*index=5*/f32[256]{0:T(256)S(1)}, s32[]{:T(128)}) while((s32[]{:T(128)}, f32[256,256]{1,0:T(8,128)S(1)}, f32[256]{0:T(256)S(1)}, pred[]{:T(512)}, f32[256,256]{1,0:T(8,128)S(1)}, ...), condition=%wide.region_3.4_spmd.clone, body=%wide.region_2.3_spmd.clone.sunk | while | flops 202375936 | bytes 3159159 | solution.py:172
  487.8 21.9 %while.96 = (s32[]{:T(128)}, f32[256]{0:T(256)S(1)}, f32[16,256]{1,0:T(8,128)S(1)}, f32[16,256,256]{2,1,0:T(8,128)}, f32[16,256]{1,0:T(8,128)S(1)}, /*index=5*/s32[]{:T(128)}, s32[]{:T(128)}) while((s32[]{:T(128)}, f32[256]{0:T(256)S(1)}, f32[16,256]{1,0:T(8,128)S(1)}, f32[16,256,256]{2,1,0:T(8,128)}, f32[16,256]{1,0:T(8,128)S(1)}, ...), condition=%wide.region_5.6_spmd, body=%wide.region_4.5_spmd.sunk | while | flops 786690 | bytes 271957 | solution.py:94
  537.6 88.0 %while.100 = (s32[]{:T(128)}, f32[256,256]{1,0:T(8,128)S(1)}, f32[256,256]{1,0:T(8,128)S(1)}, f32[256]{0:T(256)S(1)}, f32[16,256,256]{2,1,0:T(8,128)}, /*index=5...) while((s32[]{:T(128)}, f32[256,256]{1,0:T(8,128)S(1)}, ...), condition=%wide.region_7.8_spmd.clone, body=%wide.region_6.7_spmd.clone.sunk | while | flops 604897792 | bytes 3418252 | solution.py:104
  625.7 446.2 %while.101 = (s32[]{:T(128)}, f32[256,256]{1,0:T(8,128)S(1)}, f32[256,256]{1,0:T(8,128)S(1)}, f32[256]{0:T(256)S(1)}, pred[]{:T(512)}, /*index=5*/f32[256,256]{1...) while((s32[]{:T(128)}, f32[256,256]{1,0:T(8,128)S(1)}, ...), condition=%wide.region_9.10_spmd.clone, body=%wide.region_8.9_spmd.clone.sunk | while | flops 605422592 | bytes 7091353 | solution.py:186
  629.4 11.5 collective-permute-done.1
  644.5 10.8 collective-permute-done.1
  658.9 10.8 collective-permute-done.1
  673.3 10.8 collective-permute-done.1
  687.6 10.8 collective-permute-done.1
  702.0 10.8 collective-permute-done.1
  716.3 10.8 collective-permute-done.1
  730.7 10.8 collective-permute-done.1
  773.8 10.8 collective-permute-done.1
  845.6 10.8 collective-permute-done.1
  874.3 10.8 collective-permute-done.1
  888.7 10.8 collective-permute-done.1
  903.0 10.8 collective-permute-done.1
  931.8 10.8 collective-permute-done.1
  946.1 10.8 collective-permute-done.1
  960.5 10.8 collective-permute-done.1
  974.8 10.8 collective-permute-done.1
  1074.3 77.6 %while.97 = (s32[]{:T(128)}, f32[256,256]{1,0:T(8,128)S(1)}, f32[256]{0:T(256)S(1)}, f32[16,256]{1,0:T(8,128)S(1)}, f32[16,256,256]{2,1,0:T(8,128)}, /*index=5*/...) while((s32[]{:T(128)}, f32[256,256]{1,0:T(8,128)S(1)}, ...), condition=%wide.region_11.12_spmd, body=%wide.region_10.11_spmd.sunk | while | flops 403505408 | bytes 2369673 | solution.py:119
  (1001 shorter events, 871.6 us)
Async XLA Ops:
  7.2 502.7 %all-gather.4.cloned.1.call-start = ((), (), s32[]{:S(2)}) async-start(), calls=%async_computation.1 | async-start | bytes 5242880 | tf_op jit(solution)/shard_map/all_gather | solution.py:155
  16.3 91.5 %all-to-all-start = ((f32[4,16,64,256]{3,2,1,0:T(8,128)}), f32[4,16,64,256]{3,2,1,0:T(8,128)}, u32[]{:S(2)}, u32[]{:S(2)}) async-start(f32[4,16,64,256]{3,2,1,0:T(8,128)} %stack.2), calls=%async_computation | async-start | bytes 8388608 | tf_op jit(solution)/shard_map/all_to_all | solution.py:12
  21.5 496.8 %all-gather.6.cloned.1.call-start = ((), (), s32[]{:S(2)}) async-start(), calls=%async_computation.2 | async-start | bytes 5242880 | tf_op jit(solution)/shard_map/all_gather | solution.py:156
  627.5 13.5 %collective-permute-start.1 = (f32[513,256]{1,0:T(8,128)S(1)}, f32[513,256]{1,0:T(8,128)S(1)}, u32[]{:S(2)}, u32[]{:S(2)}) collective-permute-start(f32[513,256]{1,0:T(8,128)S(1)} %pad_maximum_fusion.5), channel_id=1, source_target_pairs={{4,0},{8,4},{12,8},{16,12},{20,16},{24,20},{28,24},{32,28},{36,32}... | collective-permute-start | bytes 1575944 | tf_op jit(solution)/shard_map/while/body/eval_jaxpr/ppermute | solution.py:19
  642.6 12.7 %collective-permute-start.1 = (f32[513,256]{1,0:T(8,128)S(1)}, f32[513,256]{1,0:T(8,128)S(1)}, u32[]{:S(2)}, u32[]{:S(2)}) collective-permute-start(f32[513,256]{1,0:T(8,128)S(1)} %pad_maximum_fusion.5), channel_id=1, source_target_pairs={{4,0},{8,4},{12,8},{16,12},{20,16},{24,20},{28,24},{32,28},{36,32}... | collective-permute-start | bytes 1575944 | tf_op jit(solution)/shard_map/while/body/eval_jaxpr/ppermute | solution.py:19
  657.0 12.7 %collective-permute-start.1 = (f32[513,256]{1,0:T(8,128)S(1)}, f32[513,256]{1,0:T(8,128)S(1)}, u32[]{:S(2)}, u32[]{:S(2)}) collective-permute-start(f32[513,256]{1,0:T(8,128)S(1)} %pad_maximum_fusion.5), channel_id=1, source_target_pairs={{4,0},{8,4},{12,8},{16,12},{20,16},{24,20},{28,24},{32,28},{36,32}... | collective-permute-start | bytes 1575944 | tf_op jit(solution)/shard_map/while/body/eval_jaxpr/ppermute | solution.py:19
  671.3 12.7 %collective-permute-start.1 = (f32[513,256]{1,0:T(8,128)S(1)}, f32[513,256]{1,0:T(8,128)S(1)}, u32[]{:S(2)}, u32[]{:S(2)}) collective-permute-start(f32[513,256]{1,0:T(8,128)S(1)} %pad_maximum_fusion.5), channel_id=1, source_target_pairs={{4,0},{8,4},{12,8},{16,12},{20,16},{24,20},{28,24},{32,28},{36,32}... | collective-permute-start | bytes 1575944 | tf_op jit(solution)/shard_map/while/body/eval_jaxpr/ppermute | solution.py:19
  685.7 12.7 %collective-permute-start.1 = (f32[513,256]{1,0:T(8,128)S(1)}, f32[513,256]{1,0:T(8,128)S(1)}, u32[]{:S(2)}, u32[]{:S(2)}) collective-permute-start(f32[513,256]{1,0:T(8,128)S(1)} %pad_maximum_fusion.5), channel_id=1, source_target_pairs={{4,0},{8,4},{12,8},{16,12},{20,16},{24,20},{28,24},{32,28},{36,32}... | collective-permute-start | bytes 1575944 | tf_op jit(solution)/shard_map/while/body/eval_jaxpr/ppermute | solution.py:19
  700.1 12.7 %collective-permute-start.1 = (f32[513,256]{1,0:T(8,128)S(1)}, f32[513,256]{1,0:T(8,128)S(1)}, u32[]{:S(2)}, u32[]{:S(2)}) collective-permute-start(f32[513,256]{1,0:T(8,128)S(1)} %pad_maximum_fusion.5), channel_id=1, source_target_pairs={{4,0},{8,4},{12,8},{16,12},{20,16},{24,20},{28,24},{32,28},{36,32}... | collective-permute-start | bytes 1575944 | tf_op jit(solution)/shard_map/while/body/eval_jaxpr/ppermute | solution.py:19
  714.4 12.7 %collective-permute-start.1 = (f32[513,256]{1,0:T(8,128)S(1)}, f32[513,256]{1,0:T(8,128)S(1)}, u32[]{:S(2)}, u32[]{:S(2)}) collective-permute-start(f32[513,256]{1,0:T(8,128)S(1)} %pad_maximum_fusion.5), channel_id=1, source_target_pairs={{4,0},{8,4},{12,8},{16,12},{20,16},{24,20},{28,24},{32,28},{36,32}... | collective-permute-start | bytes 1575944 | tf_op jit(solution)/shard_map/while/body/eval_jaxpr/ppermute | solution.py:19
  728.8 12.7 %collective-permute-start.1 = (f32[513,256]{1,0:T(8,128)S(1)}, f32[513,256]{1,0:T(8,128)S(1)}, u32[]{:S(2)}, u32[]{:S(2)}) collective-permute-start(f32[513,256]{1,0:T(8,128)S(1)} %pad_maximum_fusion.5), channel_id=1, source_target_pairs={{4,0},{8,4},{12,8},{16,12},{20,16},{24,20},{28,24},{32,28},{36,32}... | collective-permute-start | bytes 1575944 | tf_op jit(solution)/shard_map/while/body/eval_jaxpr/ppermute | solution.py:19
  743.1 12.7 %collective-permute-start.1 = (f32[513,256]{1,0:T(8,128)S(1)}, f32[513,256]{1,0:T(8,128)S(1)}, u32[]{:S(2)}, u32[]{:S(2)}) collective-permute-start(f32[513,256]{1,0:T(8,128)S(1)} %pad_maximum_fusion.5), channel_id=1, source_target_pairs={{4,0},{8,4},{12,8},{16,12},{20,16},{24,20},{28,24},{32,28},{36,32}... | collective-permute-start | bytes 1575944 | tf_op jit(solution)/shard_map/while/body/eval_jaxpr/ppermute | solution.py:19
  757.5 12.7 %collective-permute-start.1 = (f32[513,256]{1,0:T(8,128)S(1)}, f32[513,256]{1,0:T(8,128)S(1)}, u32[]{:S(2)}, u32[]{:S(2)}) collective-permute-start(f32[513,256]{1,0:T(8,128)S(1)} %pad_maximum_fusion.5), channel_id=1, source_target_pairs={{4,0},{8,4},{12,8},{16,12},{20,16},{24,20},{28,24},{32,28},{36,32}... | collective-permute-start | bytes 1575944 | tf_op jit(solution)/shard_map/while/body/eval_jaxpr/ppermute | solution.py:19
  771.9 12.7 %collective-permute-start.1 = (f32[513,256]{1,0:T(8,128)S(1)}, f32[513,256]{1,0:T(8,128)S(1)}, u32[]{:S(2)}, u32[]{:S(2)}) collective-permute-start(f32[513,256]{1,0:T(8,128)S(1)} %pad_maximum_fusion.5), channel_id=1, source_target_pairs={{4,0},{8,4},{12,8},{16,12},{20,16},{24,20},{28,24},{32,28},{36,32}... | collective-permute-start | bytes 1575944 | tf_op jit(solution)/shard_map/while/body/eval_jaxpr/ppermute | solution.py:19
  843.7 12.7 %collective-permute-start.1 = (f32[513,256]{1,0:T(8,128)S(1)}, f32[513,256]{1,0:T(8,128)S(1)}, u32[]{:S(2)}, u32[]{:S(2)}) collective-permute-start(f32[513,256]{1,0:T(8,128)S(1)} %pad_maximum_fusion.5), channel_id=1, source_target_pairs={{4,0},{8,4},{12,8},{16,12},{20,16},{24,20},{28,24},{32,28},{36,32}... | collective-permute-start | bytes 1575944 | tf_op jit(solution)/shard_map/while/body/eval_jaxpr/ppermute | solution.py:19
  858.0 12.7 %collective-permute-start.1 = (f32[513,256]{1,0:T(8,128)S(1)}, f32[513,256]{1,0:T(8,128)S(1)}, u32[]{:S(2)}, u32[]{:S(2)}) collective-permute-start(f32[513,256]{1,0:T(8,128)S(1)} %pad_maximum_fusion.5), channel_id=1, source_target_pairs={{4,0},{8,4},{12,8},{16,12},{20,16},{24,20},{28,24},{32,28},{36,32}... | collective-permute-start | bytes 1575944 | tf_op jit(solution)/shard_map/while/body/eval_jaxpr/ppermute | solution.py:19
  872.4 12.7 %collective-permute-start.1 = (f32[513,256]{1,0:T(8,128)S(1)}, f32[513,256]{1,0:T(8,128)S(1)}, u32[]{:S(2)}, u32[]{:S(2)}) collective-permute-start(f32[513,256]{1,0:T(8,128)S(1)} %pad_maximum_fusion.5), channel_id=1, source_target_pairs={{4,0},{8,4},{12,8},{16,12},{20,16},{24,20},{28,24},{32,28},{36,32}... | collective-permute-start | bytes 1575944 | tf_op jit(solution)/shard_map/while/body/eval_jaxpr/ppermute | solution.py:19
  886.7 12.7 %collective-permute-start.1 = (f32[513,256]{1,0:T(8,128)S(1)}, f32[513,256]{1,0:T(8,128)S(1)}, u32[]{:S(2)}, u32[]{:S(2)}) collective-permute-start(f32[513,256]{1,0:T(8,128)S(1)} %pad_maximum_fusion.5), channel_id=1, source_target_pairs={{4,0},{8,4},{12,8},{16,12},{20,16},{24,20},{28,24},{32,28},{36,32}... | collective-permute-start | bytes 1575944 | tf_op jit(solution)/shard_map/while/body/eval_jaxpr/ppermute | solution.py:19
  901.1 12.7 %collective-permute-start.1 = (f32[513,256]{1,0:T(8,128)S(1)}, f32[513,256]{1,0:T(8,128)S(1)}, u32[]{:S(2)}, u32[]{:S(2)}) collective-permute-start(f32[513,256]{1,0:T(8,128)S(1)} %pad_maximum_fusion.5), channel_id=1, source_target_pairs={{4,0},{8,4},{12,8},{16,12},{20,16},{24,20},{28,24},{32,28},{36,32}... | collective-permute-start | bytes 1575944 | tf_op jit(solution)/shard_map/while/body/eval_jaxpr/ppermute | solution.py:19
  929.8 12.7 %collective-permute-start.1 = (f32[513,256]{1,0:T(8,128)S(1)}, f32[513,256]{1,0:T(8,128)S(1)}, u32[]{:S(2)}, u32[]{:S(2)}) collective-permute-start(f32[513,256]{1,0:T(8,128)S(1)} %pad_maximum_fusion.5), channel_id=1, source_target_pairs={{4,0},{8,4},{12,8},{16,12},{20,16},{24,20},{28,24},{32,28},{36,32}... | collective-permute-start | bytes 1575944 | tf_op jit(solution)/shard_map/while/body/eval_jaxpr/ppermute | solution.py:19
  944.2 12.7 %collective-permute-start.1 = (f32[513,256]{1,0:T(8,128)S(1)}, f32[513,256]{1,0:T(8,128)S(1)}, u32[]{:S(2)}, u32[]{:S(2)}) collective-permute-start(f32[513,256]{1,0:T(8,128)S(1)} %pad_maximum_fusion.5), channel_id=1, source_target_pairs={{4,0},{8,4},{12,8},{16,12},{20,16},{24,20},{28,24},{32,28},{36,32}... | collective-permute-start | bytes 1575944 | tf_op jit(solution)/shard_map/while/body/eval_jaxpr/ppermute | solution.py:19
  958.6 12.7 %collective-permute-start.1 = (f32[513,256]{1,0:T(8,128)S(1)}, f32[513,256]{1,0:T(8,128)S(1)}, u32[]{:S(2)}, u32[]{:S(2)}) collective-permute-start(f32[513,256]{1,0:T(8,128)S(1)} %pad_maximum_fusion.5), channel_id=1, source_target_pairs={{4,0},{8,4},{12,8},{16,12},{20,16},{24,20},{28,24},{32,28},{36,32}... | collective-permute-start | bytes 1575944 | tf_op jit(solution)/shard_map/while/body/eval_jaxpr/ppermute | solution.py:19
  972.9 12.7 %collective-permute-start.1 = (f32[513,256]{1,0:T(8,128)S(1)}, f32[513,256]{1,0:T(8,128)S(1)}, u32[]{:S(2)}, u32[]{:S(2)}) collective-permute-start(f32[513,256]{1,0:T(8,128)S(1)} %pad_maximum_fusion.5), channel_id=1, source_target_pairs={{4,0},{8,4},{12,8},{16,12},{20,16},{24,20},{28,24},{32,28},{36,32}... | collective-permute-start | bytes 1575944 | tf_op jit(solution)/shard_map/while/body/eval_jaxpr/ppermute | solution.py:19
  1059.1 12.7 %collective-permute-start.1 = (f32[513,256]{1,0:T(8,128)S(1)}, f32[513,256]{1,0:T(8,128)S(1)}, u32[]{:S(2)}, u32[]{:S(2)}) collective-permute-start(f32[513,256]{1,0:T(8,128)S(1)} %pad_maximum_fusion.5), channel_id=1, source_target_pairs={{4,0},{8,4},{12,8},{16,12},{20,16},{24,20},{28,24},{32,28},{36,32}... | collective-permute-start | bytes 1575944 | tf_op jit(solution)/shard_map/while/body/eval_jaxpr/ppermute | solution.py:19
  (52 other events, 1105.2 us)
Sparse Core Ops, SparseCore 0:
  9.7 95.7 all-gather.3
  107.2 47.0 all-gather.5
